TPU v7x, 512 devices: a whole 4x4x16 slice. The times are simulated.
512 devices in a mesh: node: 64 (over z_hi, y, x, core), local: 8 (over z_lo).
Axes of the slice: x: 4, y: 4, z: 16 (z_hi: 2, z_lo: 8; z = z_hi * 8 + z_lo), core: 2. Of those that a mesh axis runs over, the one named last changes fastest.
Arguments:
- tokens: bfloat16 [65536, 8192], P(('node', 'local')), may hold values from -24 to 24
- norm_gain: bfloat16 [8192], replicated, may hold values from 0.099609375 to 1.8984375
- key_weight: bfloat16 [8192, 128], P(('node', 'local')), may hold values from -0.0625 to 0.0625
- key_cotangent: bfloat16 [65536, 128], P(('node', 'local')), may hold values from -6 to 6
Outputs:
- keys: bfloat16 [65536, 128], P(('node', 'local'))
- token_grad: bfloat16 [65536, 8192], P(('node', 'local'))
- weight_grad: float32 [8192, 128], P(('node', 'local'))
- gain_grad: float32 [8192], replicated
All inputs are finite; a program needn't handle non-finite values.
Results may differ from a plain program's by a relative error of at most 0.005.
Values may be sent and summed in bfloat16 or wider, within the bound.
No kernel may reach another device: no remote copies, remote signals or barrier semaphores. Data moves between devices by JAX's collectives and lax.ppermute only.
A program may use at most 64 MiB of HBM per device.

v0:
```python
import math

import jax
import jax.numpy as jnp
from jax import lax
from jax.sharding import PartitionSpec as P


def local(tokens, norm_gain, key_weight, key_cotangent):
    nodes = lax.axis_size("node")
    locals_count = lax.axis_size("local")
    rows_dev = key_weight.shape[0]
    width = tokens.shape[1]
    tok_rows = tokens.shape[0]
    scale = 1.0 / math.sqrt(tok_rows * nodes * locals_count)
    gain_wide = norm_gain.astype(jnp.float32)
    wide = tokens.astype(jnp.float32)
    rstd = lax.rsqrt(jnp.mean(wide * wide, axis=1, keepdims=True) + 1e-05)
    normed = wide * rstd
    hidden = (normed * gain_wide).astype(jnp.bfloat16)
    secondary = lax.all_gather(key_weight, "node", axis=0, tiled=True)
    permuted = (
        hidden.reshape(tok_rows, nodes, locals_count, rows_dev)
        .transpose(0, 2, 1, 3)
        .reshape(tok_rows, width)
    )
    whole = lax.all_gather(secondary, "local", axis=0, tiled=True)
    keys_wide = jnp.dot(permuted, whole, preferred_element_type=jnp.float32)
    dpermuted = lax.dot_general(
        key_cotangent, whole, (((1,), (1,)), ((), ())), preferred_element_type=jnp.float32
    )
    keys = keys_wide.astype(jnp.bfloat16)
    dhidden = (
        dpermuted.reshape(tok_rows, locals_count, nodes, rows_dev)
        .transpose(0, 2, 1, 3)
        .reshape(tok_rows, width)
    )
    dnormed = dhidden * gain_wide
    inner = jnp.mean(dnormed * normed, axis=1, keepdims=True)
    token_grad = (rstd * (dnormed - normed * inner)).astype(jnp.bfloat16)
    gain_terms = jnp.sum(dhidden * normed, axis=0) * scale
    gain_grad = lax.psum(gain_terms, ("node", "local"))
    partial_grad = lax.psum_scatter(
        lax.dot_general(
            permuted, key_cotangent, (((0,), (0,)), ((), ())), preferred_element_type=jnp.float32
        )
        * scale,
        "local",
        scatter_dimension=0,
        tiled=True,
    )
    weight_grad = lax.psum_scatter(partial_grad, "node", scatter_dimension=0, tiled=True)
    return (keys, token_grad, weight_grad, gain_grad)


def solution(mesh):
    placed = (
        P(("node", "local"), None),
        P(),
        P(("node", "local"), None),
        P(("node", "local"), None),
    )
    return jax.shard_map(
        local,
        mesh=mesh,
        in_specs=placed,
        out_specs=(
            P(("node", "local"), None),
            P(("node", "local"), None),
            P(("node", "local"), None),
            P(),
        ),
        check_vma=False,
    )
```

profile of v0, /device:TPU:1, one launch (start us, length us, event | category | flops | bytes accessed | tf_op | source)
XLA Modules:
  0.0 917.4 jit_solution(14104093076151203116)
XLA Ops:
  7.2 0.0 copy-start
  7.2 0.0 copy-start.1
  7.2 0.0 all-gather.2.cloned.1.call-start
  7.2 171.8 %all_gather.6 = bf16[1024,128]{1,0:T(8,128)(2,1)} all-gather(bf16[16,128]{1,0:T(8,128)(2,1)} %param.6), channel_id=1, replica_groups=mesh['node'=64,'local'=8] {'node'}, dimensions={0}, use_global_device_ids=true | all-gather | bytes 266240 | tf_op jit(solution)/shard_map/all_gather | solution.py:21
  179.0 0.0 all-gather.2.cloned.1.call-update
  179.1 0.0 reduce-scatter.3.cloned.1.call-start
  179.1 3.2 copy.9
  182.3 0.0 copy-done.1
  182.4 1.1 fusion.10
  183.5 49.9 %all-gather.2.cloned.1.call-done = bf16[8192,128]{1,0:T(8,128)(2,1)} async-done(((bf16[1024,128]{1,0:T(8,128)(2,1)}), bf16[8192,128]{1,0:T(8,128)(2,1)}) %all-gather.2.cloned.1.call-update) | async-done | bytes 2097168 | tf_op jit(solution)/shard_map/all_gather | solution.py:27
  233.3 0.0 copy-done
  233.3 2.3 fusion.11
  235.6 0.6 copy.12
  236.2 2.6 fusion.9
  238.9 4.4 fusion.8
  243.3 0.4 copy.10
  243.7 2.6 convolution_multiply_fusion
  246.3 0.0 reduce-scatter.3.cloned.1.call-update
  246.3 0.0 reduce-scatter.5.cloned.1.call-start
  246.4 104.9 %reduce-scatter.3.cloned.1.call-done = f32[1024,128]{1,0:T(8,128)} async-done(((f32[8192,128]{1,0:T(8,128)}), f32[1024,128]{1,0:T(8,128)}) %reduce-scatter.3.cloned.1.call-update) | async-done | bytes 524304 | tf_op jit(solution)/shard_map/reduce_scatter | solution.py:43
  351.2 0.0 reduce-scatter.5.cloned.1.call-update
  351.3 4.1 copy.13
  355.3 104.8 %psum.7 = f32[8192]{0:T(1024)} all-reduce(f32[8192]{0:T(1024)S(1)} %broadcast_multiply_fusion), channel_id=1, replica_groups=mesh['node'=64,'local'=8] {'node','local'}, use_global_device_ids=true, to_apply=%region_5.0 | all-reduce | flops 8192 | bytes 65536 | tf_op jit(solution)/shard_map/psum | solution.py:42
  460.2 3.0 convolution_convert_fusion
  463.1 447.7 %reduce-scatter.5.cloned.1.call-done = f32[16,128]{1,0:T(8,128)} async-done(((f32[1024,128]{1,0:T(8,128)}), f32[16,128]{1,0:T(8,128)}) %reduce-scatter.5.cloned.1.call-update) | async-done | bytes 8208 | tf_op jit(solution)/shard_map/reduce_scatter | solution.py:52
  (4 shorter events, 0.0 us)
Async XLA Ops:
  7.2 226.2 %copy-start = (bf16[128,128]{1,0:T(8,128)(2,1)S(1)}, bf16[128,128]{1,0:T(8,128)(2,1)}, u32[]{:S(2)}) copy-start(bf16[128,128]{1,0:T(8,128)(2,1)} %param.7) | copy-start | bytes 98308
  7.2 175.2 %copy-start.1 = (bf16[8192]{0:T(1024)(128)(2,1)S(1)}, bf16[8192]{0:T(1024)(128)(2,1)}, u32[]{:S(2)}) copy-start(bf16[8192]{0:T(1024)(128)(2,1)} %param.5) | copy-start | bytes 49156
  7.2 226.1 %all-gather.2.cloned.1.call-start = ((), (), s32[]{:S(2)}) async-start(), calls=%async_computation.2 | async-start | bytes 2359296 | tf_op jit(solution)/shard_map/all_gather | solution.py:27
  179.1 172.2 %reduce-scatter.3.cloned.1.call-start = ((), (), s32[]{:S(2)}) async-start(), calls=%async_computation.3 | async-start | bytes 4718592 | tf_op jit(solution)/shard_map/reduce_scatter | solution.py:43
  246.3 664.5 %reduce-scatter.5.cloned.1.call-start = ((), (), s32[]{:S(2)}) async-start(), calls=%async_computation.4 | async-start | bytes 532480 | tf_op jit(solution)/shard_map/reduce_scatter | solution.py:52
Sparse Core Ops, SparseCore 0:
  179.2 54.0 all-gather.1
  246.4 104.7 reduce-scatter.2
  354.6 556.1 reduce-scatter.4
where the time goes:
time: 930 us; the launch traced here: 917 us
  waiting for transfers between devices  602 us (65%)
  blocking collectives  277 us (30%)
  between operations  13.8 us (1%)
    reduce_scatter x1, waiting for transfers between devices, local(): lax.psum_scatter(partial_grad, 'node', scatter_dimension=0, tiled=True)  448 us
    all_gather x1, blocking collectives, local(): secondary = lax.all_gather(key_weight, 'node', axis=0, tiled=True)  172 us
    reduce_scatter x1, waiting for transfers between devices, local(): lax.psum_scatter(lax.dot_general(permuted, key_cotangent, (((0,), (0,)),...  105 us
    psum x1, blocking collectives, local(): gain_grad = lax.psum(gain_terms, ('node', 'local'))  105 us
    all_gather x1, waiting for transfers between devices, local(): whole = lax.all_gather(secondary, 'local', axis=0, tiled=True)  49.9 us
  transfers between devices with their start and end apart: 3, of which 3 were waited for; matrix products, arithmetic and copies ran while one was open for 1% of the time, Pallas kernels for 0%

commit v1 on v0

v1 whole, which is shorter than its diff:
```python
import math

import jax
import jax.numpy as jnp
from jax import lax
from jax.sharding import Mesh, PartitionSpec as P

AXES = ("zh", "y", "x", "c", "zl")
SIZES = (2, 4, 4, 2, 8)
ALONG_Z = ("zh", "zl")
PLANE = ("y", "x")
F32 = jnp.float32


def spread(block, axes, count):
    return lax.all_to_all(
        jnp.broadcast_to(block[None], (count, *block.shape)), axes, 0, 0
    )


def local(tokens, norm_gain, key_weight, key_cotangent):
    rows, width = tokens.shape
    depth = key_weight.shape[1]
    scale = 1.0 / math.sqrt(rows * 512)
    gain_wide = norm_gain.astype(F32)
    wide = tokens.astype(F32)
    rstd = lax.rsqrt(jnp.mean(wide * wide, axis=1, keepdims=True) + 1e-05)
    normed = wide * rstd
    hidden = (normed * gain_wide).astype(jnp.bfloat16)

    halves = hidden.reshape(rows, 2, 16, 2, 128).transpose(3, 0, 2, 1, 4).reshape(2, rows, 4096)
    cots = jnp.broadcast_to(key_cotangent[None], (2, rows, depth))
    pair = lax.all_to_all(jnp.concatenate([halves, cots], axis=2), "c", 0, 0)
    pair = pair.reshape(2 * rows, 4096 + depth)
    part = lax.dot_general(
        pair[:, :4096], pair[:, 4096:], (((0,), (0,)), ((), ())), preferred_element_type=F32
    )

    column = spread(key_weight, ALONG_Z, 16).reshape(256, depth)
    both = jnp.concatenate(
        [
            jnp.broadcast_to(column[None], (16, 256, depth)),
            part.astype(jnp.bfloat16).reshape(16, 256, depth),
        ],
        axis=1,
    )
    both = lax.all_to_all(both, PLANE, 0, 0)
    half_weight = both[:, :256]
    plane_sum = jnp.sum(both[:, 256:].astype(F32), axis=0)

    index = lax.axis_index(PLANE) * 2 + lax.axis_index("c")
    gain_rows = lax.dynamic_slice_in_dim(
        gain_wide.reshape(2, 32, 128), index, 1, axis=1
    ).reshape(256)
    gain_part = jnp.sum(plane_sum * column.astype(F32), axis=1) / gain_rows
    high = gain_part.astype(jnp.bfloat16)
    low = (gain_part - high.astype(F32)).astype(jnp.bfloat16)
    tail = jnp.concatenate([high, low]).reshape(1, 4, 128)
    blocks = jnp.concatenate(
        [
            plane_sum.astype(jnp.bfloat16).reshape(16, 16, 128),
            jnp.broadcast_to(tail, (16, 4, 128)),
            jnp.zeros((16, 12, 128), jnp.bfloat16),
        ],
        axis=1,
    )
    blocks = lax.all_to_all(blocks, ALONG_Z, 0, 0)
    summed = jnp.sum(blocks.astype(F32), axis=0)
    weight_grad = summed[:16] * scale
    gain_sum = (summed[16:18] + summed[18:20]) * scale
    gain_all = spread(gain_sum, ("y", "x", "c"), 32)
    gain_grad = gain_all.reshape(32, 2, 128).transpose(1, 0, 2).reshape(width)

    whole = spread(half_weight.reshape(4096, depth), "c", 2)
    whole = whole.reshape(2, 16, 2, 128, depth).transpose(2, 1, 0, 3, 4).reshape(width, depth)
    keys = jnp.dot(hidden, whole, preferred_element_type=F32).astype(jnp.bfloat16)
    dhidden = lax.dot_general(
        key_cotangent, whole, (((1,), (1,)), ((), ())), preferred_element_type=F32
    )
    dnormed = dhidden * gain_wide
    inner = jnp.mean(dnormed * normed, axis=1, keepdims=True)
    token_grad = (rstd * (dnormed - normed * inner)).astype(jnp.bfloat16)
    return (keys, token_grad, weight_grad, gain_grad)


def solution(mesh):
    fine = Mesh(mesh.devices.reshape(SIZES), AXES)
    placed = (P(AXES, None), P(), P(AXES, None), P(AXES, None))
    return jax.shard_map(
        local,
        mesh=fine,
        in_specs=placed,
        out_specs=(P(AXES, None), P(AXES, None), P(AXES, None), P()),
        check_vma=False,
    )
```

time: 930 us -> 134 us (0.14); the launches traced: 917 us -> 133 us
  waiting for transfers between devices: 602 us -> 40 us
  blocking collectives: 277 us -> 12.8 us
  starting transfers between devices: 0.12 us -> 40 us
  between operations: 13.8 us -> 0.85 us
  local copies, waits for them, and re-layouts: 8.29 us -> 20.7 us
    reduce_scatter x2 -> x0, waiting for transfers between devices: 553 us -> none  [the longest x1 448 us: local(): lax.psum_scatter(partial_grad, 'node', scatter_dimension=0, tiled=True)]
    all_gather x1 -> x0, blocking collectives: 172 us -> none  [local(): secondary = lax.all_gather(key_weight, 'node', axis=0, tiled=True)]
    psum x1 -> x0, blocking collectives: 105 us -> none  [local(): gain_grad = lax.psum(gain_terms, ('node', 'local'))]
    all_gather x1 -> x0, waiting for transfers between devices: 49.9 us -> none  [local(): whole = lax.all_gather(secondary, 'local', axis=0, tiled=True)]
    all_to_all x0 -> x5, waiting for transfers between devices: none -> 40 us  [the longest x1 26.3 us: local(): both = lax.all_to_all(both, PLANE, 0, 0)]
    all_to_all x0 -> x5, starting transfers between devices: none -> 40 us  [the longest x3 26 us: spread(): lax.all_to_all(jnp.broadcast_to(block[None], (count, *block.shape)), axes...]
    all_to_all x0 -> x1, blocking collectives: none -> 12.8 us  [local(): pair = lax.all_to_all(jnp.concatenate([halves, cots], axis=2), 'c', 0, 0)]
  transfers between devices with their start and end apart: 3 -> 5, of which waited for: 3 -> 4; matrix products, arithmetic and copies ran while one was open for 1% -> 15% of each run, Pallas kernels for 0% -> 0%
where the time goes in v1:
time: 134 us; the launch traced here: 133 us
  starting transfers between devices  40 us (30%)
  waiting for transfers between devices  40 us (30%)
  local copies, waits for them, and re-layouts  20.7 us (15%)
  blocking collectives  12.8 us (10%)
  other arithmetic  11.9 us (9%)
  matrix products  6.63 us (5%)
    all_to_all x1, waiting for transfers between devices, local(): both = lax.all_to_all(both, PLANE, 0, 0)  26.3 us
    all_to_all x3, starting transfers between devices, spread(): lax.all_to_all(jnp.broadcast_to(block[None], (count, *block.shape)), axes...  26 us
    all_to_all x3, waiting for transfers between devices, spread(): lax.all_to_all(jnp.broadcast_to(block[None], (count, *block.shape)), axes...  13.7 us
    all_to_all x1, blocking collectives, local(): pair = lax.all_to_all(jnp.concatenate([halves, cots], axis=2), 'c', 0, 0)  12.8 us
    unnamed x13, local copies, waits for them, and re-layouts  9.64 us
    all_to_all x1, starting transfers between devices, local(): blocks = lax.all_to_all(blocks, ALONG_Z, 0, 0)  7.2 us
    all_to_all x1, starting transfers between devices, local(): both = lax.all_to_all(both, PLANE, 0, 0)  6.81 us
    all_to_all x1, local copies, waits for them, and re-layouts, local(): pair = lax.all_to_all(jnp.concatenate([halves, cots], axis=2), 'c', 0, 0)  4.2 us
  transfers between devices with their start and end apart: 5, of which 4 were waited for; matrix products, arithmetic and copies ran while one was open for 15% of the time, Pallas kernels for 0%

profile of v1, /device:TPU:1, one launch (start us, length us, event | category | flops | bytes accessed | tf_op | source)
XLA Modules:
  0.0 132.9 jit_solution(17549703372583291216)
XLA Ops:
  0.6 0.7 convert_element_type.46
  1.4 0.9 copy.22
  2.2 3.2 %copy.20 = bf16[128,8192]{0,1:T(8,128)(2,1)S(1)} copy(bf16[128,8192]{1,0:T(8,128)(2,1)} %param.4) | data formatting | bytes 4194304 | tf_op args[0]
  5.5 1.1 fusion.9
  6.6 3.5 %fusion.4 = bf16[128,8192]{0,1:T(8,128)(2,1)S(1)} fusion(bf16[128,8192]{0,1:T(8,128)(2,1)S(1)} %copy.20, f32[8192]{0:T(1024)S(1)} %convert_element_type.46, f32[128]{0:T(128)S(1)} %add_rsqrt_fusion), kind=kLoop, calls=%fused_computation.8 | loop fusion | flops 4194304 | bytes 4227584 | tf_op jit(solution)/shard_map/convert_element_type | solution.py:29
  10.0 0.0 copy-start.2
  10.1 1.3 copy-done.2
  11.4 0.1 copy.21
  11.5 0.1 pad_maximum_fusion
  11.7 0.0 copy-start.4
  11.7 12.8 %all_to_all.30 = bf16[2,128,4224]{1,2,0:T(8,128)(2,1)} all-to-all(bf16[2,128,4224]{1,2,0:T(8,128)(2,1)S(1)} %pad_maximum_fusion), channel_id=1, replica_groups=mesh['zh'=2,'y'=4,'x'=4,'c'=2,'zl'=8] {'c'}, dimensions={0} | all-to-all | bytes 4325376 | tf_op jit(solution)/shard_map/all_to_all | solution.py:33
  24.5 0.0 copy-done.4
  24.5 0.6 broadcast_in_dim.18
  25.1 9.6 %all-to-all-start = ((bf16[16,16,128]{2,1,0:T(8,128)(2,1)}), bf16[16,16,128]{2,1,0:T(8,128)(2,1)S(1)}, u32[]{:S(2)}, u32[]{:S(2)}) async-start(bf16[16,16,128]{2,1,0:T(8,128)(2,1)} %broadcast_in_dim.18), calls=%async_computation | async-start | bytes 131072 | tf_op jit(solution)/shard_map/all_to_all | solution.py:16
  34.7 4.2 %copy.23 = bf16[2,128,4224]{2,1,0:T(8,128)(2,1)} copy(bf16[2,128,4224]{1,2,0:T(8,128)(2,1)} %all_to_all.30) | data formatting | bytes 4325376 | tf_op jit(solution)/shard_map/all_to_all | solution.py:33
  38.9 2.4 %convolution_convert_fusion = bf16[4096,128]{1,0:T(8,128)(2,1)S(1)} fusion(bf16[256,4224]{1,0:T(8,128)(2,1)} %bitcast.30), kind=kOutput, calls=%fused_computation.7 | convolution fusion | flops 268959744 | bytes 3211264 | tf_op jit(solution)/shard_map/dot_general | solution.py:35
  41.3 5.1 %all-to-all-done = bf16[16,16,128]{2,1,0:T(8,128)(2,1)S(1)} async-done(((bf16[16,16,128]{2,1,0:T(8,128)(2,1)}), bf16[16,16,128]{2,1,0:T(8,128)(2,1)S(1)}, u32[]{:S(2)}, u32[]{:S(2)}) %all-to-all-start) | async-done | bytes 65568 | tf_op jit(solution)/shard_map/all_to_all | solution.py:16
  46.4 0.2 broadcast_in_dim.20
  46.6 1.5 %pad_maximum_fusion.1 = bf16[16,512,128]{2,1,0:T(8,128)(2,1)} fusion(bf16[16,256,128]{2,1,0:T(8,128)(2,1)S(1)} %bitcast.32, bf16[16,256,128]{2,1,0:T(8,128)(2,1)S(1)} %broadcast_in_dim.20), kind=kLoop, calls=%fused_computation.16 | loop fusion | flops 4194304 | bytes 4194304 | tf_op jit(solution)/shard_map/concatenate | solution.py:40
  48.1 6.8 %all-to-all-start.2 = ((bf16[16,512,128]{2,1,0:T(8,128)(2,1)}), bf16[16,512,128]{2,1,0:T(8,128)(2,1)}, u32[]{:S(2)}, u32[]{:S(2)}) async-start(bf16[16,512,128]{2,1,0:T(8,128)(2,1)} %pad_maximum_fusion.1), calls=%async_computation.2 | async-start | bytes 4194304 | tf_op jit(solution)/shard_map/all_to_all | solution.py:47
  54.9 0.1 pad.2.clone
  55.0 26.3 %all-to-all-done.2 = bf16[16,512,128]{2,1,0:T(8,128)(2,1)} async-done(((bf16[16,512,128]{2,1,0:T(8,128)(2,1)}), bf16[16,512,128]{2,1,0:T(8,128)(2,1)}, u32[]{:S(2)}, u32[]{:S(2)}) %all-to-all-start.2) | async-done | bytes 2097184 | tf_op jit(solution)/shard_map/all_to_all | solution.py:47
  81.3 1.4 %convert_reduce_fusion = f32[256,128]{1,0:T(8,128)S(1)} fusion(bf16[16,512,128]{2,1,0:T(8,128)(2,1)} %all-to-all-done.2), kind=kLoop, calls=%fused_computation.17 | loop fusion | flops 1015808 | bytes 1179648 | tf_op jit(solution)/shard_map/reduce_sum | solution.py:49
  82.7 0.1 multiply_reduce_fusion
  82.8 0.1 reduce_sum.54
  82.9 1.3 slice.30
  84.2 1.5 %broadcast_in_dim.23 = bf16[2,4096,128]{2,1,0:T(8,128)(2,1)} broadcast(bf16[4096,128]{1,0:T(8,128)(2,1)S(1)} %bitcast.29), dimensions={1,2} | broadcast | bytes 3145728 | tf_op jit(solution)/shard_map/broadcast_in_dim | solution.py:17
  85.6 9.9 %all-to-all-start.3 = ((bf16[2,4096,128]{2,1,0:T(8,128)(2,1)}), bf16[2,4096,128]{2,1,0:T(8,128)(2,1)}, u32[]{:S(2)}, u32[]{:S(2)}) async-start(bf16[2,4096,128]{2,1,0:T(8,128)(2,1)} %broadcast_in_dim.23), calls=%async_computation.3 | async-start | bytes 4194304 | tf_op jit(solution)/shard_map/all_to_all | solution.py:16
  95.6 0.7 maximum_maximum_fusion
  96.3 1.9 %all-to-all-done.3 = bf16[2,4096,128]{2,1,0:T(8,128)(2,1)} async-done(((bf16[2,4096,128]{2,1,0:T(8,128)(2,1)}), bf16[2,4096,128]{2,1,0:T(8,128)(2,1)}, u32[]{:S(2)}, u32[]{:S(2)}) %all-to-all-start.3) | async-done | bytes 2097184 | tf_op jit(solution)/shard_map/all_to_all | solution.py:16
  98.2 7.2 %all-to-all-start.4 = ((bf16[16,32,128]{2,1,0:T(8,128)(2,1)}), bf16[16,32,128]{2,1,0:T(8,128)(2,1)S(1)}, u32[]{:S(2)}, u32[]{:S(2)}) async-start(bf16[16,32,128]{2,1,0:T(8,128)(2,1)} %maximum_maximum_fusion), calls=%async_computation.4 | async-start | bytes 262144 | tf_op jit(solution)/shard_map/all_to_all | solution.py:67
  105.4 0.0 copy-start.3
  105.4 1.7 %copy.24 = bf16[2,16,2,128,128]{4,3,2,1,0:T(8,128)(2,1)S(1)} copy(bf16[2,16,2,128,128]{4,3,0,1,2:T(8,128)(2,1)} %bitcast.8) | data formatting | bytes 4194304 | tf_op jit(solution)/shard_map/transpose | solution.py:75
  107.1 0.0 copy-start
  107.2 0.0 copy-done.3
  107.2 1.3 fusion.5
  108.5 0.0 copy-done
  108.5 2.1 %fusion.8 = bf16[128,8192]{0,1:T(8,128)(2,1)} fusion(f32[128,8192]{0,1:T(8,128)S(1)} %get-tuple-element.23, bf16[128,8192]{0,1:T(8,128)(2,1)S(1)} %copy.20, f32[128]{0:T(128)S(1)} %broadcast_multiply_fusion, f32[128]{0:T(128)S(1)} %add_rsqrt_fusion), kind=kLoop, calls=%fused_computation.12 | loop fusion | flops 6291456 | bytes 8389632 | tf_op jit(solution)/shard_map/convert_element_type | solution.py:82
  110.6 0.0 copy-start.1
  110.6 4.2 %copy.26 = bf16[128,8192]{1,0:T(8,128)(2,1)} copy(bf16[128,8192]{0,1:T(8,128)(2,1)} %fusion.8) | data formatting | bytes 4194304
  114.8 0.0 copy-done.1
  114.8 3.0 %convolution_convert_fusion.1 = bf16[128,128]{1,0:T(8,128)(2,1)} fusion(bf16[128,8192]{0,1:T(8,128)(2,1)} %copy-done.2, bf16[8192,128]{1,0:T(8,128)(2,1)S(1)} %bitcast.26), kind=kOutput, calls=%fused_computation.18 | convolution fusion | flops 268451840 | bytes 4227072 | tf_op jit(solution)/shard_map/dot_general | solution.py:76
  117.8 0.0 all-to-all-done.4
  117.8 0.6 broadcast_in_dim.52
  118.5 6.5 %all-to-all-start.5 = ((f32[32,2,128]{2,1,0:T(2,128)}), f32[32,2,128]{2,1,0:T(2,128)S(1)}, u32[]{:S(2)}, u32[]{:S(2)}) async-start(f32[32,2,128]{2,1,0:T(2,128)} %broadcast_in_dim.52), calls=%async_computation.5 | async-start | bytes 65536 | tf_op jit(solution)/shard_map/all_to_all | solution.py:16
  124.9 0.6 slice_multiply_fusion
  125.6 6.8 %all-to-all-done.5 = f32[32,2,128]{2,1,0:T(2,128)S(1)} async-done(((f32[32,2,128]{2,1,0:T(2,128)}), f32[32,2,128]{2,1,0:T(2,128)S(1)}, u32[]{:S(2)}, u32[]{:S(2)}) %all-to-all-start.5) | async-done | bytes 32800 | tf_op jit(solution)/shard_map/all_to_all | solution.py:16
  132.3 0.6 copy.25
  (11 shorter events, 0.1 us)
Async XLA Ops:
  10.0 1.3 %copy-start.2 = (bf16[128,8192]{0,1:T(8,128)(2,1)}, bf16[128,8192]{0,1:T(8,128)(2,1)S(1)}, u32[]{:S(2)}) copy-start(bf16[128,8192]{0,1:T(8,128)(2,1)S(1)} %fusion.4) | copy-start | bytes 6291460
  11.7 12.8 %copy-start.4 = (bf16[16,128]{1,0:T(8,128)(2,1)S(1)}, bf16[16,128]{1,0:T(8,128)(2,1)}, u32[]{:S(2)}) copy-start(bf16[16,128]{1,0:T(8,128)(2,1)} %param.6) | copy-start | bytes 12292
  25.1 21.3 %all-to-all-start = ((bf16[16,16,128]{2,1,0:T(8,128)(2,1)}), bf16[16,16,128]{2,1,0:T(8,128)(2,1)S(1)}, u32[]{:S(2)}, u32[]{:S(2)}) async-start(bf16[16,16,128]{2,1,0:T(8,128)(2,1)} %broadcast_in_dim.18), calls=%async_computation | async-start | bytes 131072 | tf_op jit(solution)/shard_map/all_to_all | solution.py:16
  48.1 33.2 %all-to-all-start.2 = ((bf16[16,512,128]{2,1,0:T(8,128)(2,1)}), bf16[16,512,128]{2,1,0:T(8,128)(2,1)}, u32[]{:S(2)}, u32[]{:S(2)}) async-start(bf16[16,512,128]{2,1,0:T(8,128)(2,1)} %pad_maximum_fusion.1), calls=%async_computation.2 | async-start | bytes 4194304 | tf_op jit(solution)/shard_map/all_to_all | solution.py:47
  85.6 12.5 %all-to-all-start.3 = ((bf16[2,4096,128]{2,1,0:T(8,128)(2,1)}), bf16[2,4096,128]{2,1,0:T(8,128)(2,1)}, u32[]{:S(2)}, u32[]{:S(2)}) async-start(bf16[2,4096,128]{2,1,0:T(8,128)(2,1)} %broadcast_in_dim.23), calls=%async_computation.3 | async-start | bytes 4194304 | tf_op jit(solution)/shard_map/all_to_all | solution.py:16
  98.2 19.6 %all-to-all-start.4 = ((bf16[16,32,128]{2,1,0:T(8,128)(2,1)}), bf16[16,32,128]{2,1,0:T(8,128)(2,1)S(1)}, u32[]{:S(2)}, u32[]{:S(2)}) async-start(bf16[16,32,128]{2,1,0:T(8,128)(2,1)} %maximum_maximum_fusion), calls=%async_computation.4 | async-start | bytes 262144 | tf_op jit(solution)/shard_map/all_to_all | solution.py:67
  105.4 1.8 %copy-start.3 = (bf16[128,128]{1,0:T(8,128)(2,1)S(1)}, bf16[128,128]{1,0:T(8,128)(2,1)}, u32[]{:S(2)}) copy-start(bf16[128,128]{1,0:T(8,128)(2,1)} %param.7) | copy-start | bytes 98308
  107.1 1.3 %copy-start = (bf16[2,16,2,128,128]{4,3,2,1,0:T(8,128)(2,1)}, bf16[2,16,2,128,128]{4,3,2,1,0:T(8,128)(2,1)S(1)}, u32[]{:S(2)}) copy-start(bf16[2,16,2,128,128]{4,3,2,1,0:T(8,128)(2,1)S(1)} %copy.24) | copy-start | bytes 6291460
  110.6 4.2 %copy-start.1 = (bf16[2,16,2,128,128]{4,3,2,1,0:T(8,128)(2,1)S(1)}, bf16[2,16,2,128,128]{4,3,2,1,0:T(8,128)(2,1)}, u32[]{:S(2)}) copy-start(bf16[2,16,2,128,128]{4,3,2,1,0:T(8,128)(2,1)} %copy-done) | copy-start | bytes 6291460
  118.5 13.8 %all-to-all-start.5 = ((f32[32,2,128]{2,1,0:T(2,128)}), f32[32,2,128]{2,1,0:T(2,128)S(1)}, u32[]{:S(2)}, u32[]{:S(2)}) async-start(f32[32,2,128]{2,1,0:T(2,128)} %broadcast_in_dim.52), calls=%async_computation.5 | async-start | bytes 65536 | tf_op jit(solution)/shard_map/all_to_all | solution.py:16

commit v2 on v1

v2 whole, which is shorter than its diff:
```python
import math

import jax
import jax.numpy as jnp
from jax import lax
from jax.experimental import pallas as pl
from jax.experimental.pallas import tpu as pltpu
from jax.sharding import Mesh, PartitionSpec as P

AXES = ("zh", "y", "x", "c", "zl")
SIZES = (2, 4, 4, 2, 8)
ALONG_Z = ("zh", "zl")
PLANE = ("y", "x")
F32 = jnp.float32
BF16 = jnp.bfloat16
LANES = 128
HALF = 4096


def lanes_at(offset):
    return pl.ds(pl.multiple_of(offset, LANES), LANES)


def norm_kernel(core_ref, tok_ref, gain_ref, cot_ref, own_ref, send_ref, rstd_ref):
    core = core_ref[0]
    wide = tok_ref[...].astype(F32)
    rstd = lax.rsqrt(jnp.mean(wide * wide, axis=1, keepdims=True) + 1e-05)
    rstd_ref[...] = jnp.broadcast_to(rstd, rstd_ref.shape)
    for zh in range(2):
        for p in range(16):
            to = (p * 2 + zh) * LANES
            for half, out_ref in ((core, own_ref), (1 - core, send_ref)):
                at = lanes_at(((zh * 16 + p) * 2 + half) * LANES)
                normed = tok_ref[:, at].astype(F32) * rstd
                out_ref[:, to : to + LANES] = (normed * gain_ref[:, at].astype(F32)).astype(BF16)
    own_ref[:, HALF:] = cot_ref[...]
    send_ref[:, HALF:] = cot_ref[...]


def norm_and_pack(core, tokens, gain_row, cots):
    rows, width = tokens.shape
    step = 32
    return pl.pallas_call(
        norm_kernel,
        grid=(rows // step,),
        in_specs=[
            pl.BlockSpec(memory_space=pltpu.SMEM),
            pl.BlockSpec((step, width), lambda i: (i, 0)),
            pl.BlockSpec((1, width), lambda i: (0, 0)),
            pl.BlockSpec((step, LANES), lambda i: (i, 0)),
        ],
        out_specs=[
            pl.BlockSpec((step, HALF + LANES), lambda i: (i, 0)),
            pl.BlockSpec((step, HALF + LANES), lambda i: (i, 0)),
            pl.BlockSpec((step, LANES), lambda i: (i, 0)),
        ],
        out_shape=[
            jax.ShapeDtypeStruct((rows, HALF + LANES), BF16),
            jax.ShapeDtypeStruct((rows, HALF + LANES), BF16),
            jax.ShapeDtypeStruct((rows, LANES), F32),
        ],
        cost_estimate=pl.CostEstimate(flops=6 << 20, bytes_accessed=4 << 20, transcendentals=128),
    )(core, tokens, gain_row, cots)


def token_kernel(
    core_ref, tok_ref, gain_ref, cot_ref, rstd_ref, own_ref, send_ref, near_ref, far_ref, keys_ref, out_ref, inner_ref
):
    core = core_ref[0]
    step = pl.program_id(0)

    @pl.when(step == 0)
    def _():
        acc = jnp.dot(own_ref[:, :HALF], near_ref[...], preferred_element_type=F32)
        acc += jnp.dot(send_ref[:, :HALF], far_ref[...], preferred_element_type=F32)
        keys_ref[...] = acc.astype(BF16)
        total = jnp.sum(acc * cot_ref[...].astype(F32), axis=1, keepdims=True)
        inner_ref[...] = jnp.broadcast_to(total * (1.0 / 8192), inner_ref.shape)

    rstd = rstd_ref[...]
    pull = rstd * rstd * inner_ref[...]
    per_step = out_ref.shape[1] // 256
    for k in range(per_step):
        m = step * per_step + k
        j = lax.rem(m, 16) * 2 + lax.div(m, 16)
        rows = pl.ds(pl.multiple_of(j * LANES, LANES), LANES)
        for half, weight_ref in ((core, near_ref), (1 - core, far_ref)):
            at = lanes_at(k * 256 + half * LANES)
            dhidden = lax.dot_general(
                cot_ref[...], weight_ref[rows, :], (((1,), (1,)), ((), ())), preferred_element_type=F32
            )
            gain = gain_ref[:, at].astype(F32)
            wide = tok_ref[:, at].astype(F32)
            out_ref[:, at] = (rstd * (dhidden * gain) - wide * pull).astype(BF16)


def keys_and_token_grad(core, tokens, gain_row, cots, rstd, own, send, near, far):
    rows, width = tokens.shape
    step = 1024
    whole = lambda *shape: pl.BlockSpec(shape, lambda i: (0,) * len(shape))
    return pl.pallas_call(
        token_kernel,
        grid=(width // step,),
        in_specs=[
            pl.BlockSpec(memory_space=pltpu.SMEM),
            pl.BlockSpec((rows, step), lambda i: (0, i)),
            pl.BlockSpec((1, step), lambda i: (0, i)),
            whole(rows, LANES),
            whole(rows, LANES),
            whole(*own.shape),
            whole(*send.shape),
            whole(*near.shape),
            whole(*far.shape),
        ],
        out_specs=[
            whole(rows, LANES),
            pl.BlockSpec((rows, step), lambda i: (0, i)),
        ],
        out_shape=[
            jax.ShapeDtypeStruct((rows, LANES), BF16),
            jax.ShapeDtypeStruct((rows, width), BF16),
        ],
        scratch_shapes=[pltpu.VMEM((rows, LANES), F32)],
        cost_estimate=pl.CostEstimate(flops=512 << 20, bytes_accessed=8 << 20, transcendentals=0),
    )(core, tokens, gain_row, cots, rstd, own, send, near, far)


def outer(packed):
    return lax.dot_general(
        packed[:, :HALF], packed[:, HALF:], (((0,), (0,)), ((), ())), preferred_element_type=F32
    )


def spread(block, axes, count):
    return lax.all_to_all(
        jnp.broadcast_to(block[None], (count, *block.shape)), axes, 0, 0
    )


def layer(tokens, norm_gain, key_weight, key_cotangent):
    rows, width = tokens.shape
    depth = key_weight.shape[1]
    scale = 1.0 / math.sqrt(rows * 512)
    gain_row = norm_gain.reshape(1, width)

    core = lax.axis_index("c").astype(jnp.int32).reshape(1)
    swap = [(0, 1), (1, 0)]

    column = spread(key_weight, ALONG_Z, 16).reshape(256, depth)
    own, send, rstd = norm_and_pack(core, tokens, gain_row, key_cotangent)
    other = lax.ppermute(send, "c", swap)
    near = spread(column, PLANE, 16).reshape(HALF, depth)
    part = outer(own) + outer(other)
    part = part.astype(BF16).reshape(16, 256, depth)
    part = lax.all_to_all(part, PLANE, 0, 0)
    far = lax.ppermute(near, "c", swap)
    keys, token_grad = keys_and_token_grad(
        core, tokens, gain_row, key_cotangent, rstd, own, send, near, far
    )

    plane_sum = jnp.sum(part.astype(F32), axis=0)
    index = lax.axis_index(PLANE) * 2 + lax.axis_index("c")
    gain_rows = lax.dynamic_slice_in_dim(
        norm_gain.astype(F32).reshape(2, 32, 128), index, 1, axis=1
    ).reshape(256)
    gain_part = jnp.sum(plane_sum * column.astype(F32), axis=1) / gain_rows
    high = gain_part.astype(BF16)
    low = (gain_part - high.astype(F32)).astype(BF16)
    tail = jnp.concatenate([high, low]).reshape(1, 4, 128)
    blocks = jnp.concatenate(
        [
            plane_sum.astype(BF16).reshape(16, 16, 128),
            jnp.broadcast_to(tail, (16, 4, 128)),
            jnp.zeros((16, 4, 128), BF16),
        ],
        axis=1,
    )
    blocks = lax.all_to_all(blocks, ALONG_Z, 0, 0)
    summed = jnp.sum(blocks.astype(F32), axis=0)
    weight_grad = summed[:16] * scale
    gain_sum = (summed[16:18] + summed[18:20]) * scale
    gain_all = spread(gain_sum, ("y", "x", "c"), 32)
    gain_grad = gain_all.reshape(32, 2, 128).transpose(1, 0, 2).reshape(width)
    return (keys, token_grad, weight_grad, gain_grad)


def solution(mesh):
    fine = Mesh(mesh.devices.reshape(SIZES), AXES)
    placed = (P(AXES, None), P(), P(AXES, None), P(AXES, None))
    return jax.shard_map(
        layer,
        mesh=fine,
        in_specs=placed,
        out_specs=(P(AXES, None), P(AXES, None), P(AXES, None), P()),
        check_vma=False,
    )
```

time: 134 us -> 114 us (0.85)
  local copies, waits for them, and re-layouts: 20.7 us -> 4.94 us
  Pallas kernels: 0 us -> 13.3 us
  other arithmetic: 11.9 us -> 2.32 us
  waiting for transfers between devices: 40 us -> 30.6 us
  blocking collectives: 12.8 us -> 21 us
  matrix products: 6.63 us -> 1.94 us
  starting transfers between devices: 40 us -> 38.4 us
    all_to_all x2, waiting for transfers between devices: 26.3 us -> 10.9 us  [the longest x1 9.03 us: layer(): part = lax.all_to_all(part, PLANE, 0, 0)]
    ppermute x0 -> x2, starting transfers between devices: none -> 13.5 us  [the longest x1 8.74 us: layer(): other = lax.ppermute(send, 'c', swap)]
    pallas_call x0 -> x2, Pallas kernels: none -> 13.3 us  [the longest x1 8.97 us: keys_and_token_grad(): pl.pallas_call(token_kernel, grid=(width // step,), in_specs=[pl.BlockSpe...]
    all_to_all x3 -> x2, starting transfers between devices: 26 us -> 15.2 us  [spread(): lax.all_to_all(jnp.broadcast_to(block[None], (count, *block.shape)), axes...]
    unnamed x13 -> x8, local copies, waits for them, and re-layouts: 9.64 us -> 1 us
    all_to_all x1, blocking collectives: 12.8 us -> 21 us  [spread(): lax.all_to_all(jnp.broadcast_to(block[None], (count, *block.shape)), axes...]
    convert_element_type x5 -> x2, other arithmetic: 6.35 us -> 0.02 us  [the longest x1 0.01 us: layer(): plane_sum.astype(BF16).reshape(16, 16, 128)]
    all_to_all x3 -> x2, waiting for transfers between devices: 13.7 us -> 19.8 us  [spread(): lax.all_to_all(jnp.broadcast_to(block[None], (count, *block.shape)), axes...]
  transfers between devices with their start and end apart: 5 -> 6, of which waited for: 4 -> 4; matrix products, arithmetic and copies ran while one was open for 15% -> 5% of each run, Pallas kernels for 0% -> 8%
where the time goes in v2:
time: 114 us; the launch traced here: 113 us
  starting transfers between devices  38.4 us (34%)
  waiting for transfers between devices  30.6 us (27%)
  blocking collectives  21 us (18%)
  Pallas kernels  13.3 us (12%)
  local copies, waits for them, and re-layouts  4.94 us (4%)
  other arithmetic  2.32 us (2%)
  matrix products  1.94 us (2%)
    all_to_all x1, blocking collectives, spread(): lax.all_to_all(jnp.broadcast_to(block[None], (count, *block.shape)), axes...  21 us
    all_to_all x2, waiting for transfers between devices, spread(): lax.all_to_all(jnp.broadcast_to(block[None], (count, *block.shape)), axes...  19.8 us
    all_to_all x2, starting transfers between devices, spread(): lax.all_to_all(jnp.broadcast_to(block[None], (count, *block.shape)), axes...  15.2 us
    all_to_all x1, waiting for transfers between devices, layer(): part = lax.all_to_all(part, PLANE, 0, 0)  9.03 us
    pallas_call x1, Pallas kernels, keys_and_token_grad(): pl.pallas_call(token_kernel, grid=(width // step,), in_specs=[pl.BlockSpe...  8.97 us
    ppermute x1, starting transfers between devices, layer(): other = lax.ppermute(send, 'c', swap)  8.74 us
    all_to_all x1, starting transfers between devices, layer(): blocks = lax.all_to_all(blocks, ALONG_Z, 0, 0)  5.33 us
    ppermute x1, starting transfers between devices, layer(): far = lax.ppermute(near, 'c', swap)  4.8 us
  transfers between devices with their start and end apart: 6, of which 4 were waited for; matrix products, arithmetic and copies ran while one was open for 5% of the time, Pallas kernels for 8%

profile of v2, /device:TPU:1, one launch (start us, length us, event | category | flops | bytes accessed | tf_op | source)
XLA Modules:
  0.0 113.3 jit_solution(14862750931479433220)
XLA Ops:
  0.6 1.4 %reshape.49.gain_ref = bf16[1,8192]{1,0:T(2,128)(2,1)} reshape(bf16[8192]{0:T(1024)(128)(2,1)} %param.5) | data formatting | bytes 32768 | tf_op jit(solution)/shard_map/reshape | solution.py:144
  2.0 0.0 copy-start.3
  2.0 4.3 %shard_map.75 = (bf16[128,4224]{1,0:T(8,128)(2,1)}, bf16[128,4224]{1,0:T(8,128)(2,1)}, f32[128,128]{1,0:T(8,128)}) custom-call(s32[1]{0:T(128)} %bitcast.core_ref, bf16[128,8192]{1,0:T(8,128)(2,1)} %tok_ref.3, bf16[1,8192]{1,0:T(2,128)(2,1)} %reshape.49.gain_ref, bf16[128,128]{1,0:T(8,128)(2,1)} %cot_ref.3), custom_call_target="tpu_custom_call" | custom-call | flops 6291456 | bytes 4194304 | tf_op jit(solution)/shard_map/pallas_call | solution.py:43
  6.3 8.7 %collective-permute-start.1 = (bf16[128,4224]{1,0:T(8,128)(2,1)}, bf16[128,4224]{1,0:T(8,128)(2,1)S(1)}, u32[]{:S(2)}, u32[]{:S(2)}) collective-permute-start(bf16[128,4224]{1,0:T(8,128)(2,1)} %get-tuple-element.11.send_ref), channel_id=1, source_target_pairs={{0,8},{8,0},{1,9},{9,1},{2,10},{10,2},{3,11},{11,3},{4,12},{12,4},... | collective-permute-start | bytes 3244040 | tf_op jit(solution)/shard_map/ppermute | solution.py:151
  15.0 0.0 copy-done.3
  15.1 21.0 %all_to_all.25 = bf16[16,16,128]{2,1,0:T(8,128)(2,1)S(1)} all-to-all(bf16[16,16,128]{2,1,0:T(8,128)(2,1)S(1)} %broadcast_in_dim.12), channel_id=1, replica_groups=mesh['zh'=2,'y'=4,'x'=4,'c'=2,'zl'=8] {'zh','zl'}, dimensions={0} | all-to-all | bytes 131072 | tf_op jit(solution)/shard_map/all_to_all | solution.py:135
  36.1 1.2 %broadcast_in_dim.14 = bf16[16,256,128]{2,1,0:T(8,128)(2,1)} broadcast(bf16[256,128]{1,0:T(8,128)(2,1)S(1)} %bitcast.15), dimensions={1,2} | broadcast | bytes 1114112 | tf_op jit(solution)/shard_map/broadcast_in_dim | solution.py:136
  37.2 0.0 copy-start
  37.2 6.9 %all-to-all-start.1 = ((bf16[16,256,128]{2,1,0:T(8,128)(2,1)}), bf16[16,256,128]{2,1,0:T(8,128)(2,1)S(1)}, u32[]{:S(2)}, u32[]{:S(2)}) async-start(bf16[16,256,128]{2,1,0:T(8,128)(2,1)} %broadcast_in_dim.14), calls=%async_computation.1 | async-start | bytes 2097152 | tf_op jit(solution)/shard_map/all_to_all | solution.py:135
  44.1 0.0 copy-done
  44.1 0.5 fusion.2
  44.6 0.0 collective-permute-done.1
  44.6 1.5 %fusion = bf16[4096,128]{1,0:T(8,128)(2,1)} fusion(f32[4096,128]{1,0:T(8,128)S(1)} %fusion.2, bf16[128,4224]{1,0:T(8,128)(2,1)S(1)} %collective-permute-done.1), kind=kOutput, calls=%fused_computation.1 | convolution fusion | flops 135266304 | bytes 4227072 | tf_op jit(solution)/shard_map/dot_general | solution.py:129
  46.1 13.0 %all-to-all-done.1 = bf16[16,256,128]{2,1,0:T(8,128)(2,1)S(1)} async-done(((bf16[16,256,128]{2,1,0:T(8,128)(2,1)}), bf16[16,256,128]{2,1,0:T(8,128)(2,1)S(1)}, u32[]{:S(2)}, u32[]{:S(2)}) %all-to-all-start.1) | async-done | bytes 1048608 | tf_op jit(solution)/shard_map/all_to_all | solution.py:135
  59.1 0.0 copy-start.1
  59.1 4.3 %all-to-all-start.2 = ((bf16[16,256,128]{2,1,0:T(8,128)(2,1)}), bf16[16,256,128]{2,1,0:T(8,128)(2,1)S(1)}, u32[]{:S(2)}, u32[]{:S(2)}) async-start(bf16[16,256,128]{2,1,0:T(8,128)(2,1)} %bitcast.3), calls=%async_computation.2 | async-start | bytes 2097152 | tf_op jit(solution)/shard_map/all_to_all | solution.py:155
  63.4 0.1 pad.2.clone
  63.5 0.7 dynamic-slice_convert_fusion
  64.2 4.8 %collective-permute-start = (bf16[4096,128]{1,0:T(8,128)(2,1)S(1)}, bf16[4096,128]{1,0:T(8,128)(2,1)S(1)}, u32[]{:S(2)}, u32[]{:S(2)}) collective-permute-start(bf16[4096,128]{1,0:T(8,128)(2,1)S(1)} %bitcast.12), channel_id=1, source_target_pairs={{0,8},{8,0},{1,9},{9,1},{2,10},{10,2},{3,11},{11,3},{4,12},{12,4},... | collective-permute-start | bytes 3145736 | tf_op jit(solution)/shard_map/ppermute | solution.py:156
  69.0 9.0 %all-to-all-done.2 = bf16[16,256,128]{2,1,0:T(8,128)(2,1)S(1)} async-done(((bf16[16,256,128]{2,1,0:T(8,128)(2,1)}), bf16[16,256,128]{2,1,0:T(8,128)(2,1)S(1)}, u32[]{:S(2)}, u32[]{:S(2)}) %all-to-all-start.2) | async-done | bytes 1048608 | tf_op jit(solution)/shard_map/all_to_all | solution.py:155
  78.0 0.1 convert_reduce_fusion
  78.2 0.0 copy-done.1
  78.2 0.1 multiply_reduce_fusion
  78.3 0.1 reduce_sum.34
  78.4 0.7 maximum_maximum_fusion
  79.2 5.3 %all-to-all-start.3 = ((bf16[16,24,128]{2,1,0:T(8,128)(2,1)}), bf16[16,24,128]{2,1,0:T(8,128)(2,1)S(1)}, u32[]{:S(2)}, u32[]{:S(2)}) async-start(bf16[16,24,128]{2,1,0:T(8,128)(2,1)} %maximum_maximum_fusion), calls=%async_computation.3 | async-start | bytes 196608 | tf_op jit(solution)/shard_map/all_to_all | solution.py:178
  84.5 0.0 collective-permute-done.far_ref
  84.5 0.0 copy-start.2
  84.5 1.0 copy-done.2
  85.5 9.0 %shard_map.76 = (bf16[128,128]{1,0:T(8,128)(2,1)}, bf16[128,8192]{1,0:T(8,128)(2,1)}) custom-call(s32[1]{0:T(128)} %bitcast.core_ref, bf16[128,8192]{1,0:T(8,128)(2,1)} %tok_ref.3, bf16[1,8192]{1,0:T(2,128)(2,1)} %reshape.49.gain_ref, bf16[128,128]{1,0:T(8,128)(2,1)} %cot_ref.3, f32[128,128]{1,0:T(8,128)} %get-tuple-element.9.rstd_ref, ...), custom_call_target="tpu_custom_call" | custom-call | flops 536870912 | bytes 8388608 | tf_op jit(solution)/shard_map/pallas_call | solution.py:101
  94.5 1.9 %all-to-all-done.3 = bf16[16,24,128]{2,1,0:T(8,128)(2,1)S(1)} async-done(((bf16[16,24,128]{2,1,0:T(8,128)(2,1)}), bf16[16,24,128]{2,1,0:T(8,128)(2,1)S(1)}, u32[]{:S(2)}, u32[]{:S(2)}) %all-to-all-start.3) | async-done | bytes 98336 | tf_op jit(solution)/shard_map/all_to_all | solution.py:178
  96.4 0.6 broadcast_in_dim.32
  97.0 8.3 %all-to-all-start.4 = ((f32[32,2,128]{2,1,0:T(2,128)}), f32[32,2,128]{2,1,0:T(2,128)S(1)}, u32[]{:S(2)}, u32[]{:S(2)}) async-start(f32[32,2,128]{2,1,0:T(2,128)} %broadcast_in_dim.32), calls=%async_computation.4 | async-start | bytes 65536 | tf_op jit(solution)/shard_map/all_to_all | solution.py:135
  105.3 0.6 slice_multiply_fusion
  105.9 6.8 %all-to-all-done.4 = f32[32,2,128]{2,1,0:T(2,128)S(1)} async-done(((f32[32,2,128]{2,1,0:T(2,128)}), f32[32,2,128]{2,1,0:T(2,128)S(1)}, u32[]{:S(2)}, u32[]{:S(2)}) %all-to-all-start.4) | async-done | bytes 32800 | tf_op jit(solution)/shard_map/all_to_all | solution.py:135
  112.7 0.6 copy.8
  (8 shorter events, 0.1 us)
Async XLA Ops:
  2.0 13.0 %copy-start.3 = (bf16[16,128]{1,0:T(8,128)(2,1)S(1)}, bf16[16,128]{1,0:T(8,128)(2,1)}, u32[]{:S(2)}) copy-start(bf16[16,128]{1,0:T(8,128)(2,1)} %param.6) | copy-start | bytes 12292
  6.3 38.3 %collective-permute-start.1 = (bf16[128,4224]{1,0:T(8,128)(2,1)}, bf16[128,4224]{1,0:T(8,128)(2,1)S(1)}, u32[]{:S(2)}, u32[]{:S(2)}) collective-permute-start(bf16[128,4224]{1,0:T(8,128)(2,1)} %get-tuple-element.11.send_ref), channel_id=1, source_target_pairs={{0,8},{8,0},{1,9},{9,1},{2,10},{10,2},{3,11},{11,3},{4,12},{12,4},... | collective-permute-start | bytes 3244040 | tf_op jit(solution)/shard_map/ppermute | solution.py:151
  37.2 6.9 %copy-start = (bf16[128,4224]{1,0:T(8,128)(2,1)S(1)}, bf16[128,4224]{1,0:T(8,128)(2,1)}, u32[]{:S(2)}) copy-start(bf16[128,4224]{1,0:T(8,128)(2,1)} %get-tuple-element.10.own_ref) | copy-start | bytes 3244036
  37.2 21.8 %all-to-all-start.1 = ((bf16[16,256,128]{2,1,0:T(8,128)(2,1)}), bf16[16,256,128]{2,1,0:T(8,128)(2,1)S(1)}, u32[]{:S(2)}, u32[]{:S(2)}) async-start(bf16[16,256,128]{2,1,0:T(8,128)(2,1)} %broadcast_in_dim.14), calls=%async_computation.1 | async-start | bytes 2097152 | tf_op jit(solution)/shard_map/all_to_all | solution.py:135
  59.1 19.1 %copy-start.1 = (bf16[16,256,128]{2,1,0:T(8,128)(2,1)}, bf16[16,256,128]{2,1,0:T(8,128)(2,1)S(1)}, u32[]{:S(2)}) copy-start(bf16[16,256,128]{2,1,0:T(8,128)(2,1)S(1)} %all-to-all-done.1) | copy-start | bytes 3145732
  59.1 18.9 %all-to-all-start.2 = ((bf16[16,256,128]{2,1,0:T(8,128)(2,1)}), bf16[16,256,128]{2,1,0:T(8,128)(2,1)S(1)}, u32[]{:S(2)}, u32[]{:S(2)}) async-start(bf16[16,256,128]{2,1,0:T(8,128)(2,1)} %bitcast.3), calls=%async_computation.2 | async-start | bytes 2097152 | tf_op jit(solution)/shard_map/all_to_all | solution.py:155
  64.2 20.3 %collective-permute-start = (bf16[4096,128]{1,0:T(8,128)(2,1)S(1)}, bf16[4096,128]{1,0:T(8,128)(2,1)S(1)}, u32[]{:S(2)}, u32[]{:S(2)}) collective-permute-start(bf16[4096,128]{1,0:T(8,128)(2,1)S(1)} %bitcast.12), channel_id=1, source_target_pairs={{0,8},{8,0},{1,9},{9,1},{2,10},{10,2},{3,11},{11,3},{4,12},{12,4},... | collective-permute-start | bytes 3145736 | tf_op jit(solution)/shard_map/ppermute | solution.py:156
  79.2 17.2 %all-to-all-start.3 = ((bf16[16,24,128]{2,1,0:T(8,128)(2,1)}), bf16[16,24,128]{2,1,0:T(8,128)(2,1)S(1)}, u32[]{:S(2)}, u32[]{:S(2)}) async-start(bf16[16,24,128]{2,1,0:T(8,128)(2,1)} %maximum_maximum_fusion), calls=%async_computation.3 | async-start | bytes 196608 | tf_op jit(solution)/shard_map/all_to_all | solution.py:178
  84.5 1.0 copy-start.2
  97.0 15.7 %all-to-all-start.4 = ((f32[32,2,128]{2,1,0:T(2,128)}), f32[32,2,128]{2,1,0:T(2,128)S(1)}, u32[]{:S(2)}, u32[]{:S(2)}) async-start(f32[32,2,128]{2,1,0:T(2,128)} %broadcast_in_dim.32), calls=%async_computation.4 | async-start | bytes 65536 | tf_op jit(solution)/shard_map/all_to_all | solution.py:135
